TPU v7x, 256 devices: a whole 4x4x8 slice. The times are simulated.
256 devices in a mesh: gx: 8 (over y, z_hi), gy: 8 (over z_lo, core), gz: 4 (over x).
Axes of the slice: x: 4, y: 4, z: 8 (z_hi: 2, z_lo: 4; z = z_hi * 4 + z_lo), core: 2. Of those that a mesh axis runs over, the one named last changes fastest.
Arguments:
- right_side: float32 [3, 64, 64, 512], P(None, 'gx', 'gy', 'gz'), may hold values from -17 to 17
- phase_labels: int32 [32, 32, 256], P('gx', 'gy', 'gz'), may hold values from 0 to 7
- phase_moduli: float32 [8], replicated, may hold values from 0.03 to 0.3
- coarse_nodes: int32 [64, 64, 512], P('gx', 'gy', 'gz'), may hold values from 0 to 5
- coarse_inverse: float32 [9216, 9216], P(('gx', 'gy', 'gz')), as said below
Outputs:
- solution_field: float32 [3, 64, 64, 512], P(None, 'gx', 'gy', 'gz')
- residual: float32 [3, 64, 64, 512], P(None, 'gx', 'gy', 'gz')
Inputs may be any that keep to these rules, and one draw needn't show every extreme that they name: `coarse_inverse`: symmetric.
All inputs are finite; a program needn't handle non-finite values.
Results may differ from a plain program's by a relative error of at most 0.0003.
Values sent between devices are 32-bit elements; how exact they have to be, the bound alone decides.
A program may use at most 64 MiB of HBM per device.

v0:
```python
import jax
import jax.numpy as jnp
from jax import lax
from jax.sharding import PartitionSpec as P

SWEEPS = 4
ITERS = 2
bond_ratio = 0.5
relax = 0.6
highest = lax.Precision.HIGHEST
neighbour_offsets = tuple(
    (
        (shift_x, shift_y, shift_z)
        for shift_x in (-1, 0, 1)
        for shift_y in (-1, 0, 1)
        for shift_z in (-1, 0, 1)
        if shift_x * shift_x + shift_y * shift_y + shift_z * shift_z > 0
    )
)


def extended(x, sides, width):
    for axis, dim in sides:
        size, length = (lax.axis_size(axis), x.shape[dim])
        up = [(i, (i + 1) % size) for i in range(size - 1)]
        down = [(j, i) for i, j in up]
        last = lax.slice_in_dim(x, length - width, length, axis=dim)
        leading = lax.slice_in_dim(x, 0, width, axis=dim)
        before = lax.ppermute(last, axis, up)
        after = lax.ppermute(leading, axis, down)
        x = jnp.concatenate([before, x, after], axis=dim)
    return x


def inner_view(array, shift_x, shift_y, shift_z):
    size_x, size_y, size_z = array.shape[-3:]
    return array[
        ...,
        1 + shift_x : size_x - 1 + shift_x,
        1 + shift_y : size_y - 1 + shift_y,
        1 + shift_z : size_z - 1 + shift_z,
    ]


def spring_force(field_pad, stiff_pad):
    centre = inner_view(field_pad, 0, 0, 0)
    stiff_centre = inner_view(stiff_pad, 0, 0, 0)
    parts = [jnp.zeros_like(centre[0]) for component in range(3)]
    for offset in neighbour_offsets:
        length = offset[0] * offset[0] + offset[1] * offset[1] + offset[2] * offset[2]
        spring = (
            0.5 * (stiff_centre + inner_view(stiff_pad, offset[0], offset[1], offset[2])) / length
        )
        partner = inner_view(field_pad, offset[0], offset[1], offset[2])
        stretch = [centre[component] - partner[component] for component in range(3)]
        projected = jnp.zeros_like(stretch[0])
        for component in range(3):
            if offset[component] != 0:
                projected = projected + offset[component] * stretch[component]
        for component in range(3):
            summand = stretch[component]
            if offset[component] != 0:
                summand = summand + bond_ratio * offset[component] / length * projected
            parts[component] = parts[component] + spring * summand
    return jnp.stack(parts)


def diagonal(stiff_pad):
    stiff_centre = inner_view(stiff_pad, 0, 0, 0)
    parts = [jnp.zeros_like(stiff_centre) for component in range(3)]
    for offset in neighbour_offsets:
        length = offset[0] * offset[0] + offset[1] * offset[1] + offset[2] * offset[2]
        spring = (
            0.5 * (stiff_centre + inner_view(stiff_pad, offset[0], offset[1], offset[2])) / length
        )
        for component in range(3):
            parts[component] = parts[component] + spring * (
                1.0 + bond_ratio * offset[component] * offset[component] / length
            )
    return jnp.stack(parts)


def local_solve(residual_ext, stiff_rim, diag_ext):
    widths = [(0, 0)] * (residual_ext.ndim - 3) + [(1, 1)] * 3
    solution = relax * residual_ext / diag_ext
    for sweep in range(SWEEPS - 1):
        solution = (
            solution
            + relax * (residual_ext - spring_force(jnp.pad(solution, widths), stiff_rim)) / diag_ext
        )
    return solution


def cross(first, second):
    return jnp.stack(
        [
            first[1] * second[2] - first[2] * second[1],
            first[2] * second[0] - first[0] * second[2],
            first[0] * second[1] - first[1] * second[0],
        ]
    )


def local_coords(size_x, size_y, size_z):
    along_x = ((2.0 * jnp.arange(size_x, dtype=jnp.float32) + 1.0) / size_x - 1.0).reshape(
        size_x, 1, 1
    )
    along_y = ((2.0 * jnp.arange(size_y, dtype=jnp.float32) + 1.0) / size_y - 1.0).reshape(
        1, size_y, 1
    )
    along_z = ((2.0 * jnp.arange(size_z, dtype=jnp.float32) + 1.0) / size_z - 1.0).reshape(
        1, 1, size_z
    )
    return (along_x, along_y, along_z)


def fold_axis(spread, axis):
    size = spread.shape[axis]
    count = size - 4
    inner = lax.slice_in_dim(spread, 2, size - 2, axis=axis)
    lower = lax.slice_in_dim(spread, 0, 1, axis=axis)
    upper = lax.slice_in_dim(spread, size - 1, size, axis=axis)
    head = lax.slice_in_dim(inner, 0, 1, axis=axis) + lower
    tail = lax.slice_in_dim(inner, count - 1, count, axis=axis) + upper
    middle = lax.slice_in_dim(inner, 1, count - 1, axis=axis)
    return jnp.concatenate([head, middle, tail], axis=axis)


def body(right_side, phase_labels, phase_moduli, coarse_nodes, coarse_inverse):
    phases = phase_moduli.shape[0]
    matches = phase_labels[None] == jnp.arange(phases, dtype=jnp.int32)[:, None, None, None]
    coarse_stiff = jnp.sum(jnp.where(matches, phase_moduli[:, None, None, None], 0.0), axis=0)
    stiffness = jnp.repeat(jnp.repeat(jnp.repeat(coarse_stiff, 2, axis=0), 2, axis=1), 2, axis=2)
    stiff_rim = extended(stiffness, (("gx", 0), ("gy", 1), ("gz", 2)), 2)
    diag_ext = diagonal(stiff_rim)
    stiff_near = stiff_rim[1:-1, 1:-1, 1:-1]
    size_x, size_y, size_z = stiffness.shape
    coords = local_coords(size_x, size_y, size_z)
    node_count = coarse_inverse.shape[0] // 6
    onehot = (
        jnp.arange(node_count, dtype=jnp.int32)[:, None] == coarse_nodes.reshape(1, -1)
    ).astype(jnp.float32)

    def accumulate(piece):
        return jnp.dot(coarse_inverse, piece, precision=highest)

    def coarse_part(residual):
        moments = jnp.concatenate([residual, cross(coords, residual)], axis=0).reshape(6, -1)
        node_sums = jnp.einsum("gc,mc->gm", onehot, moments, precision=highest).reshape(-1)
        solved = accumulate(lax.all_gather(node_sums, ("gx", "gy", "gz"), axis=0, tiled=True))
        per_cell = jnp.einsum("gm,gc->mc", solved.reshape(node_count, 6), onehot, precision=highest)
        per_cell = per_cell.reshape(6, size_x, size_y, size_z)
        return per_cell[:3] + cross(per_cell[3:], coords)

    def local_part(residual_ext):
        solution = local_solve(residual_ext, stiff_rim, diag_ext)
        spread = extended(solution, (("gx", 1), ("gy", 2), ("gz", 3)), 1)
        return fold_axis(fold_axis(fold_axis(spread, 1), 2), 3)

    def widen(vector):
        return extended(vector, (("gx", 1), ("gy", 2), ("gz", 3)), 1)

    def precondition(residual_form):
        return local_part(widen(residual_form)) + coarse_part(residual_form)

    residual = right_side
    solution_field = jnp.zeros_like(right_side)

    def global_sum(value):
        return lax.psum(value, ("gx", "gy", "gz"))

    search = precondition(residual)
    norm_now = global_sum(jnp.sum(residual * search))
    direction = search
    for step in range(ITERS):
        image = spring_force(widen(direction), stiff_near)
        step_size = norm_now / global_sum(jnp.sum(direction * image))
        solution_field = solution_field + step_size * direction
        residual = residual - step_size * image
        if step + 1 < ITERS:
            search = precondition(residual)
            norm_next = global_sum(jnp.sum(residual * search))
            direction = search + norm_next / norm_now * direction
            norm_now = norm_next
    return (solution_field, residual)


def solution(mesh):
    in_specs = (
        P(None, "gx", "gy", "gz"),
        P("gx", "gy", "gz"),
        P(),
        P("gx", "gy", "gz"),
        P(("gx", "gy", "gz"), None),
    )
    out_specs = (P(None, "gx", "gy", "gz"), P(None, "gx", "gy", "gz"))
    return jax.shard_map(body, mesh=mesh, in_specs=in_specs, out_specs=out_specs, check_vma=False)
```

profile of v0, /device:TPU:1, one launch (start us, length us, event | category | flops | bytes accessed | tf_op | source)
XLA Modules:
  0.0 682.7 jit_solution(17536681381676741998)
XLA Ops:
  1.8 9.8 %collective-permute-start.6 = (f32[2,8,128]{2,1,0:T(8,128)S(1)}, f32[2,8,128]{2,1,0:T(8,128)S(1)}, u32[]{:S(2)}, u32[]{:S(2)}) collective-permute-start(f32[2,8,128]{2,1,0:T(8,128)S(1)} %broadcast_in_dim.51), channel_id=1, source_target_pairs={{0,32},{32,64},{64,96},{96,128},{128,160},{160,192},{192,224},{1,3... | collective-permute-start | bytes 24584 | tf_op jit(solution)/shard_map/ppermute | solution.py:29
  13.8 7.9 %collective-permute-start = (f32[3,1,8,128]{3,2,1,0:T(8,128)S(1)}, f32[3,1,8,128]{3,2,1,0:T(8,128)S(1)}, u32[]{:S(2)}, u32[]{:S(2)}) collective-permute-start(f32[3,1,8,128]{3,2,1,0:T(8,128)S(1)} %get-tuple-element.274), channel_id=1, source_target_pairs={{0,32},{32,64},{64,96},{96,128},{128,160},{160,192},{192,224},{1,3... | collective-permute-start | bytes 36872 | tf_op jit(solution)/shard_map/ppermute | solution.py:29
  26.5 79.8 %all-reduce.6 = f32[9216]{0:T(1024)S(1)} all-reduce(f32[9216]{0:T(1024)S(1)} %dynamic-update-slice), channel_id=1, replica_groups=mesh['gx'=8,'gy'=8,'gz'=4] {'gx','gy','gz'}, use_global_device_ids=true, to_apply=%add.6 | all-reduce | flops 9216 | bytes 73728
  109.1 3.2 collective-permute-start.8
  112.3 1.9 collective-permute-start.9
  114.3 3.0 collective-permute-done.9
  117.5 2.2 collective-permute-start.10
  121.0 2.2 collective-permute-start.2
  123.2 2.1 collective-permute-start.3
  128.4 4.3 collective-permute-start.4
  136.1 4.1 collective-permute-done.5
  140.7 1.8 fusion.1591
  144.8 2.6 fusion.1589
  147.6 1.7 fusion.1588
  151.0 1.7 fusion.1586
  152.9 2.3 fusion.1585
  157.0 1.7 fusion.1583
  159.1 5.2 collective-permute-start.12
  166.0 7.6 %collective-permute-done.13 = f32[3,1,10,130]{3,2,1,0:T(8,128)S(1)} collective-permute-done((f32[3,1,10,130]{3,2,1,0:T(8,128)S(1)}, f32[3,1,10,130]{3,2,1,0:T(8,128)S(1)}, u32[]{:S(2)}, u32[]{:S(2)}) %collective-permute-start.13) | collective-permute-done | bytes 15632 | tf_op jit(solution)/shard_map/ppermute | solution.py:30
  173.7 4.0 collective-permute-start.14
  177.7 1.9 collective-permute-start.15
  179.7 3.3 collective-permute-done.15
  183.3 2.5 collective-permute-start.16
  187.2 3.7 collective-permute-done.16
  190.9 4.1 collective-permute-done.17
  197.7 5.2 collective-permute-start.18
  204.2 7.5 %collective-permute-done.19 = f32[3,1,8,128]{3,2,1,0:T(8,128)S(1)} collective-permute-done((f32[3,1,8,128]{3,2,1,0:T(8,128)S(1)}, f32[3,1,8,128]{3,2,1,0:T(8,128)S(1)}, u32[]{:S(2)}, u32[]{:S(2)}) %collective-permute-start.19) | collective-permute-done | bytes 12320 | tf_op jit(solution)/shard_map/ppermute | solution.py:30
  211.7 5.1 collective-permute-start.20
  216.9 1.9 collective-permute-start.21
  219.0 3.0 collective-permute-done.21
  222.2 2.8 collective-permute-start.22
  226.5 6.0 collective-permute-done.23
  240.8 74.1 %all-reduce.8 = (f32[]{:T(128)}, f32[]{:T(128)}) all-reduce(f32[]{:T(128)} %get-tuple-element.29, f32[]{:T(128)} %fusion.1595), channel_id=1, replica_groups=mesh['gx'=8,'gy'=8,'gz'=4] {'gx','gy','gz'}, use_global_device_ids=true, to_apply=%region_2.3 | all-reduce | flops 2 | bytes 16 | tf_op jit(solution)/shard_map/psum | solution.py:170
  319.5 4.6 collective-permute-start.24
  325.5 1.8 fusion.28
  330.7 77.3 %all-reduce.7 = f32[9216]{0:T(1024)} all-reduce(f32[9216]{0:T(1024)} %dynamic-update-slice.1), channel_id=1, replica_groups=mesh['gx'=8,'gy'=8,'gz'=4] {'gx','gy','gz'}, use_global_device_ids=true, to_apply=%add.7 | all-reduce | flops 9216 | bytes 73728
  410.2 4.2 collective-permute-start.26
  414.4 2.6 convolution_bitcast_fusion
  418.4 2.0 collective-permute-start.27
  424.1 2.3 collective-permute-start.28
  429.7 4.1 collective-permute-done.29
  434.5 1.7 fusion.1582
  437.9 1.6 fusion.1580
  439.8 1.7 fusion.1579
  443.1 1.6 fusion.1577
  445.0 2.1 fusion.1576
  448.8 1.6 fusion.1574
  450.9 3.9 collective-permute-start.30
  457.0 7.2 %collective-permute-done.31 = f32[3,1,10,130]{3,2,1,0:T(8,128)S(1)} collective-permute-done((f32[3,1,10,130]{3,2,1,0:T(8,128)S(1)}, f32[3,1,10,130]{3,2,1,0:T(8,128)S(1)}, u32[]{:S(2)}, u32[]{:S(2)}) %collective-permute-start.31) | collective-permute-done | bytes 15632 | tf_op jit(solution)/shard_map/ppermute | solution.py:30
  464.2 4.6 collective-permute-start.32
  468.8 1.9 collective-permute-start.33
  470.8 3.3 collective-permute-done.33
  474.4 2.5 collective-permute-start.34
  478.3 3.7 collective-permute-done.34
  482.0 4.1 collective-permute-done.35
  488.8 75.1 %psum.30 = f32[]{:T(128)} all-reduce(f32[]{:T(128)} %get-tuple-element.18), channel_id=1, replica_groups=mesh['gx'=8,'gy'=8,'gz'=4] {'gx','gy','gz'}, use_global_device_ids=true, to_apply=%region_6.7 | all-reduce | flops 1 | bytes 8 | tf_op jit(solution)/shard_map/psum | solution.py:170
  565.2 5.2 collective-permute-start.36
  571.7 7.0 %collective-permute-done.37 = f32[3,1,8,128]{3,2,1,0:T(8,128)S(1)} collective-permute-done((f32[3,1,8,128]{3,2,1,0:T(8,128)S(1)}, f32[3,1,8,128]{3,2,1,0:T(8,128)S(1)}, u32[]{:S(2)}, u32[]{:S(2)}) %collective-permute-start.37) | collective-permute-done | bytes 12320 | tf_op jit(solution)/shard_map/ppermute | solution.py:30
  578.8 3.7 collective-permute-start.38
  582.5 1.9 collective-permute-start.39
  584.5 3.0 collective-permute-done.39
  587.7 2.4 collective-permute-start.40
  591.7 6.0 collective-permute-done.41
  606.7 73.8 %psum.31 = f32[]{:T(128)} all-reduce(f32[]{:T(128)} %fusion.1594), channel_id=1, replica_groups=mesh['gx'=8,'gy'=8,'gz'=4] {'gx','gy','gz'}, use_global_device_ids=true, to_apply=%region_8.9 | all-reduce | flops 1 | bytes 8 | tf_op jit(solution)/shard_map/psum | solution.py:170
  (467 shorter events, 85.9 us)
Async XLA Ops:
  0.6 105.7 %copy-start = (f32[36,9216]{1,0:T(8,128)S(1)}, f32[36,9216]{1,0:T(8,128)}, u32[]{:S(2)}) copy-start(f32[36,9216]{1,0:T(8,128)} %param.9) | copy-start | bytes 3981316
  1.8 105.9 %copy-start.120 = (s32[8,8,128]{2,1,0:T(8,128)S(1)}, s32[8,8,128]{2,1,0:T(8,128)}, u32[]{:S(2)}) copy-start(s32[8,8,128]{2,1,0:T(8,128)} %param.8) | copy-start | bytes 98308
  1.8 107.3 %collective-permute-start.6 = (f32[2,8,128]{2,1,0:T(8,128)S(1)}, f32[2,8,128]{2,1,0:T(8,128)S(1)}, u32[]{:S(2)}, u32[]{:S(2)}) collective-permute-start(f32[2,8,128]{2,1,0:T(8,128)S(1)} %broadcast_in_dim.51), channel_id=1, source_target_pairs={{0,32},{32,64},{64,96},{96,128},{128,160},{160,192},{192,224},{1,3... | collective-permute-start | bytes 24584 | tf_op jit(solution)/shard_map/ppermute | solution.py:29
  11.7 97.4 %collective-permute-start.7 = (f32[2,8,128]{2,1,0:T(8,128)S(1)}, f32[2,8,128]{2,1,0:T(8,128)S(1)}, u32[]{:S(2)}, u32[]{:S(2)}) collective-permute-start(f32[2,8,128]{2,1,0:T(8,128)S(1)} %broadcast_in_dim.59), channel_id=1, source_target_pairs={{32,0},{64,32},{96,64},{128,96},{160,128},{192,160},{224,192},{33,... | collective-permute-start | bytes 24584 | tf_op jit(solution)/shard_map/ppermute | solution.py:30
  13.8 100.5 %collective-permute-start = (f32[3,1,8,128]{3,2,1,0:T(8,128)S(1)}, f32[3,1,8,128]{3,2,1,0:T(8,128)S(1)}, u32[]{:S(2)}, u32[]{:S(2)}) collective-permute-start(f32[3,1,8,128]{3,2,1,0:T(8,128)S(1)} %get-tuple-element.274), channel_id=1, source_target_pairs={{0,32},{32,64},{64,96},{96,128},{128,160},{160,192},{192,224},{1,3... | collective-permute-start | bytes 36872 | tf_op jit(solution)/shard_map/ppermute | solution.py:29
  21.6 92.7 %collective-permute-start.1 = (f32[3,1,8,128]{3,2,1,0:T(8,128)S(1)}, f32[3,1,8,128]{3,2,1,0:T(8,128)S(1)}, u32[]{:S(2)}, u32[]{:S(2)}) collective-permute-start(f32[3,1,8,128]{3,2,1,0:T(8,128)S(1)} %get-tuple-element.273), channel_id=1, source_target_pairs={{32,0},{64,32},{96,64},{128,96},{160,128},{192,160},{224,192},{33,... | collective-permute-start | bytes 36872 | tf_op jit(solution)/shard_map/ppermute | solution.py:30
  23.0 85.7 %copy-start.124 = (f32[8]{0:T(128)}, f32[8]{0:T(128)S(1)}, u32[]{:S(2)}) copy-start(f32[8]{0:T(128)S(1)} %multiply_add_fusion.115) | copy-start | bytes 100
  23.0 85.7 %copy-start.127 = (f32[128]{0:T(128)}, f32[128]{0:T(128)S(1)}, u32[]{:S(2)}) copy-start(f32[128]{0:T(128)S(1)} %multiply_add_fusion.114) | copy-start | bytes 1540
  109.1 5.2 collective-permute-start.8
  112.3 5.0 collective-permute-start.9
  117.5 7.8 %collective-permute-start.10 = (f32[12,12,2]{2,1,0:T(8,128)S(1)}, f32[12,12,2]{2,1,0:T(8,128)S(1)}, u32[]{:S(2)}, u32[]{:S(2)}) collective-permute-start(f32[12,12,2]{2,1,0:T(8,128)S(1)} %get-tuple-element.271), channel_id=1, source_target_pairs={{0,1},{1,2},{2,3},{4,5},{5,6},{6,7},{8,9},{9,10},{10,11},{12,13},{... | collective-permute-start | bytes 3464 | tf_op jit(solution)/shard_map/ppermute | solution.py:29
  119.6 5.7 collective-permute-start.11
  121.0 6.1 collective-permute-start.2
  123.2 5.0 collective-permute-start.3
  126.3 30.5 %copy-start.1 = (f32[10,10,130]{2,1,0:T(8,128)}, f32[10,10,130]{2,1,0:T(8,128)S(1)}, u32[]{:S(2)}) copy-start(f32[10,10,130]{2,1,0:T(8,128)S(1)} %get-tuple-element.85) | copy-start | bytes 156004
  126.3 30.5 %copy-start.3 = (f32[10,10,130]{2,1,0:T(8,128)}, f32[10,10,130]{2,1,0:T(8,128)S(1)}, u32[]{:S(2)}) copy-start(f32[10,10,130]{2,1,0:T(8,128)S(1)} %get-tuple-element.86) | copy-start | bytes 156004
  126.3 30.5 %copy-start.5 = (f32[10,10,130]{2,1,0:T(8,128)}, f32[10,10,130]{2,1,0:T(8,128)S(1)}, u32[]{:S(2)}) copy-start(f32[10,10,130]{2,1,0:T(8,128)S(1)} %get-tuple-element.87) | copy-start | bytes 156004
  126.4 30.5 %copy-start.7 = (f32[10,10,130]{2,1,0:T(8,128)}, f32[10,10,130]{2,1,0:T(8,128)S(1)}, u32[]{:S(2)}) copy-start(f32[10,10,130]{2,1,0:T(8,128)S(1)} %get-tuple-element.88) | copy-start | bytes 156004
  126.4 30.5 %copy-start.9 = (f32[10,10,130]{2,1,0:T(8,128)}, f32[10,10,130]{2,1,0:T(8,128)S(1)}, u32[]{:S(2)}) copy-start(f32[10,10,130]{2,1,0:T(8,128)S(1)} %get-tuple-element.89) | copy-start | bytes 156004
  126.4 30.5 %copy-start.15 = (f32[10,10,130]{2,1,0:T(8,128)}, f32[10,10,130]{2,1,0:T(8,128)S(1)}, u32[]{:S(2)}) copy-start(f32[10,10,130]{2,1,0:T(8,128)S(1)} %get-tuple-element.71) | copy-start | bytes 156004
  126.4 30.5 %copy-start.17 = (f32[10,10,130]{2,1,0:T(8,128)}, f32[10,10,130]{2,1,0:T(8,128)S(1)}, u32[]{:S(2)}) copy-start(f32[10,10,130]{2,1,0:T(8,128)S(1)} %get-tuple-element.72) | copy-start | bytes 156004
  126.4 30.5 %copy-start.19 = (f32[10,10,130]{2,1,0:T(8,128)}, f32[10,10,130]{2,1,0:T(8,128)S(1)}, u32[]{:S(2)}) copy-start(f32[10,10,130]{2,1,0:T(8,128)S(1)} %get-tuple-element.90) | copy-start | bytes 156004
  126.4 30.5 %copy-start.21 = (f32[10,10,130]{2,1,0:T(8,128)}, f32[10,10,130]{2,1,0:T(8,128)S(1)}, u32[]{:S(2)}) copy-start(f32[10,10,130]{2,1,0:T(8,128)S(1)} %get-tuple-element.91) | copy-start | bytes 156004
  126.4 32.2 %copy-start.33 = (f32[1,10,10,130]{3,2,1,0:T(8,128)}, f32[1,10,10,130]{3,2,1,0:T(8,128)S(1)}, u32[]{:S(2)}) copy-start(f32[1,10,10,130]{3,2,1,0:T(8,128)S(1)} %get-tuple-element.70) | copy-start | bytes 156004
  127.0 29.9 %copy-start.11 = (f32[10,10,130]{2,1,0:T(8,128)}, f32[10,10,130]{2,1,0:T(8,128)S(1)}, u32[]{:S(2)}) copy-start(f32[10,10,130]{2,1,0:T(8,128)S(1)} %get-tuple-element.93) | copy-start | bytes 156004
  127.0 29.9 %copy-start.13 = (f32[10,10,130]{2,1,0:T(8,128)}, f32[10,10,130]{2,1,0:T(8,128)S(1)}, u32[]{:S(2)}) copy-start(f32[10,10,130]{2,1,0:T(8,128)S(1)} %get-tuple-element.94) | copy-start | bytes 156004
  127.0 31.6 %copy-start.29 = (f32[1,10,10,130]{3,2,1,0:T(8,128)}, f32[1,10,10,130]{3,2,1,0:T(8,128)S(1)}, u32[]{:S(2)}) copy-start(f32[1,10,10,130]{3,2,1,0:T(8,128)S(1)} %get-tuple-element.92) | copy-start | bytes 156004
  128.4 7.7 %collective-permute-start.4 = (f32[3,10,10,1]{3,0,2,1:T(4,128)S(1)}, f32[3,10,10,1]{3,0,2,1:T(4,128)S(1)}, u32[]{:S(2)}, u32[]{:S(2)}) collective-permute-start(f32[3,10,10,1]{3,0,2,1:T(4,128)S(1)} %get-tuple-element.241), channel_id=1, source_target_pairs={{0,1},{1,2},{2,3},{4,5},{5,6},{6,7},{8,9},{9,10},{10,11},{12,13},{... | collective-permute-start | bytes 3608 | tf_op jit(solution)/shard_map/ppermute | solution.py:29
  132.7 7.5 %collective-permute-start.5 = (f32[3,10,10,1]{3,0,2,1:T(4,128)S(1)}, f32[3,10,10,1]{3,0,2,1:T(4,128)S(1)}, u32[]{:S(2)}, u32[]{:S(2)}) collective-permute-start(f32[3,10,10,1]{3,0,2,1:T(4,128)S(1)} %get-tuple-element.242), channel_id=1, source_target_pairs={{1,0},{2,1},{3,2},{5,4},{6,5},{7,6},{9,8},{10,9},{11,10},{13,12},{... | collective-permute-start | bytes 3608 | tf_op jit(solution)/shard_map/ppermute | solution.py:30
  159.1 6.9 %collective-permute-start.12 = (f32[3,1,10,130]{3,2,1,0:T(8,128)S(1)}, f32[3,1,10,130]{3,2,1,0:T(8,128)S(1)}, u32[]{:S(2)}, u32[]{:S(2)}) collective-permute-start(f32[3,1,10,130]{3,2,1,0:T(8,128)S(1)} %get-tuple-element.107), channel_id=1, source_target_pairs={{0,32},{32,64},{64,96},{96,128},{128,160},{160,192},{192,224},{1,3... | collective-permute-start | bytes 46808 | tf_op jit(solution)/shard_map/ppermute | solution.py:29
  164.3 9.3 %collective-permute-start.13 = (f32[3,1,10,130]{3,2,1,0:T(8,128)S(1)}, f32[3,1,10,130]{3,2,1,0:T(8,128)S(1)}, u32[]{:S(2)}, u32[]{:S(2)}) collective-permute-start(f32[3,1,10,130]{3,2,1,0:T(8,128)S(1)} %get-tuple-element.108), channel_id=1, source_target_pairs={{32,0},{64,32},{96,64},{128,96},{160,128},{192,160},{224,192},{33,... | collective-permute-start | bytes 46808 | tf_op jit(solution)/shard_map/ppermute | solution.py:30
  166.0 74.0 %copy-start.110 = (f32[1,8192]{1,0:T(1,128)}, f32[1,8192]{1,0:T(1,128)S(1)}, u32[]{:S(2)}) copy-start(f32[1,8192]{1,0:T(1,128)S(1)} %get-tuple-element.226) | copy-start | bytes 98308
  166.0 74.0 %copy-start.112 = (f32[1,8192]{1,0:T(1,128)}, f32[1,8192]{1,0:T(1,128)S(1)}, u32[]{:S(2)}) copy-start(f32[1,8192]{1,0:T(1,128)S(1)} %get-tuple-element.227) | copy-start | bytes 98308
  166.0 74.0 %copy-start.114 = (f32[1,8192]{1,0:T(1,128)}, f32[1,8192]{1,0:T(1,128)S(1)}, u32[]{:S(2)}) copy-start(f32[1,8192]{1,0:T(1,128)S(1)} %get-tuple-element.228) | copy-start | bytes 98308
  173.7 5.9 collective-permute-start.14
  177.7 5.3 collective-permute-start.15
  183.3 7.6 %collective-permute-start.16 = (f32[3,12,12,1]{3,2,1,0:T(8,128)S(1)}, f32[3,12,12,1]{3,2,1,0:T(8,128)S(1)}, u32[]{:S(2)}, u32[]{:S(2)}) collective-permute-start(f32[3,12,12,1]{3,2,1,0:T(8,128)S(1)} %get-tuple-element.101), channel_id=1, source_target_pairs={{0,1},{1,2},{2,3},{4,5},{5,6},{6,7},{8,9},{9,10},{10,11},{12,13},{... | collective-permute-start | bytes 5192 | tf_op jit(solution)/shard_map/ppermute | solution.py:29
  185.8 9.2 %collective-permute-start.17 = (f32[3,12,12,1]{3,2,1,0:T(8,128)S(1)}, f32[3,12,12,1]{3,2,1,0:T(8,128)S(1)}, u32[]{:S(2)}, u32[]{:S(2)}) collective-permute-start(f32[3,12,12,1]{3,2,1,0:T(8,128)S(1)} %get-tuple-element.102), channel_id=1, source_target_pairs={{1,0},{2,1},{3,2},{5,4},{6,5},{7,6},{9,8},{10,9},{11,10},{13,12},{... | collective-permute-start | bytes 5192 | tf_op jit(solution)/shard_map/ppermute | solution.py:30
  197.7 42.3 %copy-start.101 = (f32[1,3,64,128]{3,2,1,0:T(8,128)}, f32[1,3,64,128]{3,2,1,0:T(8,128)S(1)}, u32[]{:S(2)}) copy-start(f32[1,3,64,128]{3,2,1,0:T(8,128)S(1)} %get-tuple-element.225) | copy-start | bytes 294916
  197.7 6.5 collective-permute-start.18
  202.9 8.8 %collective-permute-start.19 = (f32[3,1,8,128]{3,2,1,0:T(8,128)S(1)}, f32[3,1,8,128]{3,2,1,0:T(8,128)S(1)}, u32[]{:S(2)}, u32[]{:S(2)}) collective-permute-start(f32[3,1,8,128]{3,2,1,0:T(8,128)S(1)} %get-tuple-element.270), channel_id=1, source_target_pairs={{32,0},{64,32},{96,64},{128,96},{160,128},{192,160},{224,192},{33,... | collective-permute-start | bytes 36872 | tf_op jit(solution)/shard_map/ppermute | solution.py:30
  211.7 7.1 %collective-permute-start.20 = (f32[3,10,1,128]{3,2,1,0:T(1,128)S(1)}, f32[3,10,1,128]{3,2,1,0:T(1,128)S(1)}, u32[]{:S(2)}, u32[]{:S(2)}) collective-permute-start(f32[3,10,1,128]{3,2,1,0:T(1,128)S(1)} %get-tuple-element.255), channel_id=1, source_target_pairs={{0,4},{4,8},{8,12},{12,16},{16,20},{20,24},{24,28},{1,5},{5,9},{9,... | collective-permute-start | bytes 46088 | tf_op jit(solution)/shard_map/ppermute | solution.py:29
  216.9 5.0 collective-permute-start.21
  222.2 12.9 %collective-permute-start.22 = (f32[3,10,10,1]{3,0,2,1:T(4,128)S(1)}, f32[3,10,10,1]{3,0,2,1:T(4,128)S(1)}, u32[]{:S(2)}, u32[]{:S(2)}) collective-permute-start(f32[3,10,10,1]{3,0,2,1:T(4,128)S(1)} %get-tuple-element.239), channel_id=1, source_target_pairs={{0,1},{1,2},{2,3},{4,5},{5,6},{6,7},{8,9},{9,10},{10,11},{12,13},{... | collective-permute-start | bytes 3608 | tf_op jit(solution)/shard_map/ppermute | solution.py:29
  225.0 7.5 %collective-permute-start.23 = (f32[3,10,10,1]{3,0,2,1:T(4,128)S(1)}, f32[3,10,10,1]{3,0,2,1:T(4,128)S(1)}, u32[]{:S(2)}, u32[]{:S(2)}) collective-permute-start(f32[3,10,10,1]{3,0,2,1:T(4,128)S(1)} %get-tuple-element.240), channel_id=1, source_target_pairs={{1,0},{2,1},{3,2},{5,4},{6,5},{7,6},{9,8},{10,9},{11,10},{13,12},{... | collective-permute-start | bytes 3608 | tf_op jit(solution)/shard_map/ppermute | solution.py:30
  319.5 88.4 %collective-permute-start.24 = (f32[3,1,8,128]{3,2,1,0:T(8,128)}, f32[3,1,8,128]{3,2,1,0:T(8,128)}, u32[]{:S(2)}, u32[]{:S(2)}) collective-permute-start(f32[3,1,8,128]{3,2,1,0:T(8,128)} %get-tuple-element.267), channel_id=1, source_target_pairs={{0,32},{32,64},{64,96},{96,128},{128,160},{160,192},{192,224},{1,3... | collective-permute-start | bytes 36872 | tf_op jit(solution)/shard_map/ppermute | solution.py:29
  324.2 83.8 %collective-permute-start.25 = (f32[3,1,8,128]{3,2,1,0:T(8,128)}, f32[3,1,8,128]{3,2,1,0:T(8,128)}, u32[]{:S(2)}, u32[]{:S(2)}) collective-permute-start(f32[3,1,8,128]{3,2,1,0:T(8,128)} %get-tuple-element.268), channel_id=1, source_target_pairs={{32,0},{64,32},{96,64},{128,96},{160,128},{192,160},{224,192},{33,... | collective-permute-start | bytes 36872 | tf_op jit(solution)/shard_map/ppermute | solution.py:30
  410.2 10.2 %collective-permute-start.26 = (f32[3,10,1,128]{3,2,1,0:T(1,128)}, f32[3,10,1,128]{3,2,1,0:T(1,128)}, u32[]{:S(2)}, u32[]{:S(2)}) collective-permute-start(f32[3,10,1,128]{3,2,1,0:T(1,128)} %get-tuple-element.252), channel_id=1, source_target_pairs={{0,4},{4,8},{8,12},{12,16},{16,20},{20,24},{24,28},{1,5},{5,9},{9,... | collective-permute-start | bytes 46088 | tf_op jit(solution)/shard_map/ppermute | solution.py:29
  418.4 5.4 collective-permute-start.27
  424.1 5.7 collective-permute-start.28
  426.4 7.5 %collective-permute-start.29 = (f32[3,10,10,1]{3,0,2,1:T(4,128)S(1)}, f32[3,10,10,1]{3,0,2,1:T(4,128)S(1)}, u32[]{:S(2)}, u32[]{:S(2)}) collective-permute-start(f32[3,10,10,1]{3,0,2,1:T(4,128)S(1)} %get-tuple-element.238), channel_id=1, source_target_pairs={{1,0},{2,1},{3,2},{5,4},{6,5},{7,6},{9,8},{10,9},{11,10},{13,12},{... | collective-permute-start | bytes 3608 | tf_op jit(solution)/shard_map/ppermute | solution.py:30
  429.0 41.8 %copy-start.43 = (f32[6,8192]{1,0:T(8,128)}, f32[6,8192]{1,0:T(8,128)S(1)}, u32[]{:S(2)}) copy-start(f32[6,8192]{1,0:T(8,128)S(1)} %fusion.36) | copy-start | bytes 589828
  450.9 6.1 collective-permute-start.30
  454.8 9.4 %collective-permute-start.31 = (f32[3,1,10,130]{3,2,1,0:T(8,128)S(1)}, f32[3,1,10,130]{3,2,1,0:T(8,128)S(1)}, u32[]{:S(2)}, u32[]{:S(2)}) collective-permute-start(f32[3,1,10,130]{3,2,1,0:T(8,128)S(1)} %get-tuple-element.106), channel_id=1, source_target_pairs={{32,0},{64,32},{96,64},{128,96},{160,128},{192,160},{224,192},{33,... | collective-permute-start | bytes 46808 | tf_op jit(solution)/shard_map/ppermute | solution.py:30
  464.2 6.5 collective-permute-start.32
  468.8 5.3 collective-permute-start.33
  474.4 7.6 %collective-permute-start.34 = (f32[3,12,12,1]{3,2,1,0:T(8,128)S(1)}, f32[3,12,12,1]{3,2,1,0:T(8,128)S(1)}, u32[]{:S(2)}, u32[]{:S(2)}) collective-permute-start(f32[3,12,12,1]{3,2,1,0:T(8,128)S(1)} %get-tuple-element.97), channel_id=1, source_target_pairs={{0,1},{1,2},{2,3},{4,5},{5,6},{6,7},{8,9},{9,10},{10,11},{12,13},{... | collective-permute-start | bytes 5192 | tf_op jit(solution)/shard_map/ppermute | solution.py:29
  476.9 9.2 %collective-permute-start.35 = (f32[3,12,12,1]{3,2,1,0:T(8,128)S(1)}, f32[3,12,12,1]{3,2,1,0:T(8,128)S(1)}, u32[]{:S(2)}, u32[]{:S(2)}) collective-permute-start(f32[3,12,12,1]{3,2,1,0:T(8,128)S(1)} %get-tuple-element.98), channel_id=1, source_target_pairs={{1,0},{2,1},{3,2},{5,4},{6,5},{7,6},{9,8},{10,9},{11,10},{13,12},{... | collective-permute-start | bytes 5192 | tf_op jit(solution)/shard_map/ppermute | solution.py:30
  565.2 6.5 collective-permute-start.36
  570.4 8.3 %collective-permute-start.37 = (f32[3,1,8,128]{3,2,1,0:T(8,128)S(1)}, f32[3,1,8,128]{3,2,1,0:T(8,128)S(1)}, u32[]{:S(2)}, u32[]{:S(2)}) collective-permute-start(f32[3,1,8,128]{3,2,1,0:T(8,128)S(1)} %get-tuple-element.266), channel_id=1, source_target_pairs={{32,0},{64,32},{96,64},{128,96},{160,128},{192,160},{224,192},{33,... | collective-permute-start | bytes 36872 | tf_op jit(solution)/shard_map/ppermute | solution.py:30
  578.8 5.6 collective-permute-start.38
  582.5 5.0 collective-permute-start.39
  587.7 12.7 %collective-permute-start.40 = (f32[3,10,10,1]{3,0,2,1:T(4,128)S(1)}, f32[3,10,10,1]{3,0,2,1:T(4,128)S(1)}, u32[]{:S(2)}, u32[]{:S(2)}) collective-permute-start(f32[3,10,10,1]{3,0,2,1:T(4,128)S(1)} %get-tuple-element.235), channel_id=1, source_target_pairs={{0,1},{1,2},{2,3},{4,5},{5,6},{6,7},{8,9},{9,10},{10,11},{12,13},{... | collective-permute-start | bytes 3608 | tf_op jit(solution)/shard_map/ppermute | solution.py:29
  590.1 7.5 %collective-permute-start.41 = (f32[3,10,10,1]{3,0,2,1:T(4,128)S(1)}, f32[3,10,10,1]{3,0,2,1:T(4,128)S(1)}, u32[]{:S(2)}, u32[]{:S(2)}) collective-permute-start(f32[3,10,10,1]{3,0,2,1:T(4,128)S(1)} %get-tuple-element.236), channel_id=1, source_target_pairs={{1,0},{2,1},{3,2},{5,4},{6,5},{7,6},{9,8},{10,9},{11,10},{13,12},{... | collective-permute-start | bytes 3608 | tf_op jit(solution)/shard_map/ppermute | solution.py:30
  (108 other events, 602.5 us)
where the time goes:
time: 690 us; the launch traced here: 683 us
  blocking collectives  380 us (55%)
  starting transfers between devices  120 us (17%)
  waiting for transfers between devices  85.4 us (12%)
  other arithmetic  64 us (9%)
  local copies, waits for them, and re-layouts  16 us (2%)
  matrix products  9.04 us (1%)
  between operations  7.75 us (1%)
    psum x3, blocking collectives, global_sum(): return lax.psum(value, ('gx', 'gy', 'gz'))  223 us
    unnamed x2, blocking collectives  157 us
    ppermute x21, starting transfers between devices, extended(): before = lax.ppermute(last, axis, up)  87.8 us
    ppermute x21, waiting for transfers between devices, extended(): after = lax.ppermute(leading, axis, down)  76 us
    ppermute x21, starting transfers between devices, extended(): after = lax.ppermute(leading, axis, down)  32.7 us
    another operation x18, other arithmetic, spring_force(): return jnp.stack(parts)  32.1 us
    concatenate x27, other arithmetic, extended(): x = jnp.concatenate([before, x, after], axis=dim)  15.2 us
  transfers between devices with their start and end apart: 42, of which 21 were waited for; matrix products, arithmetic and copies ran while one was open for 4% of the time, Pallas kernels for 0%

commit v1 on v0

--- a/solution.py
+++ b/solution.py
@@ -167,7 +167,7 @@
     solution_field = jnp.zeros_like(right_side)
 
     def global_sum(value):
-        return lax.psum(value, ("gx", "gy", "gz"))
+        return lax.psum(lax.psum(value, "gx"), ("gy", "gz"))
 
     search = precondition(residual)
     norm_now = global_sum(jnp.sum(residual * search))

time: 690 us -> 752 us (1.090)
  blocking collectives: 380 us -> 433 us
    psum x3 -> x6, blocking collectives: 223 us -> 272 us  [global_sum(): return lax.psum(lax.psum(value, 'gx'), ('gy', 'gz'))]
where the time goes in v1:
time: 752 us; the launch traced here: 739 us
  blocking collectives  433 us (58%)
  starting transfers between devices  126 us (17%)
  waiting for transfers between devices  83.6 us (11%)
  other arithmetic  63.9 us (8%)
  local copies, waits for them, and re-layouts  16 us (2%)
  matrix products  9.02 us (1%)
  between operations  7.73 us (1%)
    psum x6, blocking collectives, global_sum(): return lax.psum(lax.psum(value, 'gx'), ('gy', 'gz'))  272 us
    unnamed x2, blocking collectives  161 us
    ppermute x21, starting transfers between devices, extended(): before = lax.ppermute(last, axis, up)  86.5 us
    ppermute x21, waiting for transfers between devices, extended(): after = lax.ppermute(leading, axis, down)  74.2 us
    ppermute x21, starting transfers between devices, extended(): after = lax.ppermute(leading, axis, down)  39.6 us
    another operation x18, other arithmetic, spring_force(): return jnp.stack(parts)  32.1 us
    concatenate x27, other arithmetic, extended(): x = jnp.concatenate([before, x, after], axis=dim)  15.2 us
  transfers between devices with their start and end apart: 42, of which 21 were waited for; matrix products, arithmetic and copies ran while one was open for 4% of the time, Pallas kernels for 0%

profile of v1, /device:TPU:1, one launch (start us, length us, event | category | flops | bytes accessed | tf_op | source)
XLA Modules:
  0.0 739.0 jit_solution(1192415692491690265)
XLA Ops:
  1.8 9.8 %collective-permute-start.6 = (f32[2,8,128]{2,1,0:T(8,128)S(1)}, f32[2,8,128]{2,1,0:T(8,128)S(1)}, u32[]{:S(2)}, u32[]{:S(2)}) collective-permute-start(f32[2,8,128]{2,1,0:T(8,128)S(1)} %broadcast_in_dim.51), channel_id=1, source_target_pairs={{0,32},{32,64},{64,96},{96,128},{128,160},{160,192},{192,224},{1,3... | collective-permute-start | bytes 24584 | tf_op jit(solution)/shard_map/ppermute | solution.py:29
  13.8 7.9 %collective-permute-start = (f32[3,1,8,128]{3,2,1,0:T(8,128)S(1)}, f32[3,1,8,128]{3,2,1,0:T(8,128)S(1)}, u32[]{:S(2)}, u32[]{:S(2)}) collective-permute-start(f32[3,1,8,128]{3,2,1,0:T(8,128)S(1)} %get-tuple-element.276), channel_id=1, source_target_pairs={{0,32},{32,64},{64,96},{96,128},{128,160},{160,192},{192,224},{1,3... | collective-permute-start | bytes 36872 | tf_op jit(solution)/shard_map/ppermute | solution.py:29
  26.5 79.8 %all-reduce.6 = f32[9216]{0:T(1024)S(1)} all-reduce(f32[9216]{0:T(1024)S(1)} %dynamic-update-slice), channel_id=1, replica_groups=mesh['gx'=8,'gy'=8,'gz'=4] {'gx','gy','gz'}, use_global_device_ids=true, to_apply=%add.6 | all-reduce | flops 9216 | bytes 73728
  109.1 3.2 collective-permute-start.8
  112.3 1.9 collective-permute-start.9
  114.3 3.0 collective-permute-done.9
  117.4 2.2 collective-permute-start.10
  120.9 2.2 collective-permute-start.2
  123.2 2.1 collective-permute-start.3
  128.4 4.3 collective-permute-start.4
  136.1 4.1 collective-permute-done.5
  140.7 1.8 fusion.1591
  144.8 2.6 fusion.1589
  147.6 1.7 fusion.1588
  151.0 1.7 fusion.1586
  152.9 2.3 fusion.1585
  157.0 1.7 fusion.1583
  159.1 5.2 collective-permute-start.12
  166.0 7.6 %collective-permute-done.13 = f32[3,1,10,130]{3,2,1,0:T(8,128)S(1)} collective-permute-done((f32[3,1,10,130]{3,2,1,0:T(8,128)S(1)}, f32[3,1,10,130]{3,2,1,0:T(8,128)S(1)}, u32[]{:S(2)}, u32[]{:S(2)}) %collective-permute-start.13) | collective-permute-done | bytes 15632 | tf_op jit(solution)/shard_map/ppermute | solution.py:30
  173.8 4.0 collective-permute-start.14
  177.7 1.9 collective-permute-start.15
  179.7 3.3 collective-permute-done.15
  183.3 2.5 collective-permute-start.16
  187.2 3.7 collective-permute-done.16
  190.9 4.1 collective-permute-done.17
  197.7 5.2 collective-permute-start.18
  204.2 7.5 %collective-permute-done.19 = f32[3,1,8,128]{3,2,1,0:T(8,128)S(1)} collective-permute-done((f32[3,1,8,128]{3,2,1,0:T(8,128)S(1)}, f32[3,1,8,128]{3,2,1,0:T(8,128)S(1)}, u32[]{:S(2)}, u32[]{:S(2)}) %collective-permute-start.19) | collective-permute-done | bytes 12320 | tf_op jit(solution)/shard_map/ppermute | solution.py:30
  211.7 5.1 collective-permute-start.20
  216.9 1.9 collective-permute-start.21
  218.9 3.0 collective-permute-done.21
  222.1 2.8 collective-permute-start.22
  226.5 6.0 collective-permute-done.23
  240.8 24.7 %all-reduce.9 = (f32[]{:T(128)}, f32[]{:T(128)}) all-reduce(f32[]{:T(128)} %get-tuple-element.31, f32[]{:T(128)} %fusion.1595), channel_id=1, replica_groups=mesh['gx'=8,'gy'=8,'gz'=4] {'gx'}, use_global_device_ids=true, to_apply=%region_2.3 | all-reduce | flops 2 | bytes 16 | tf_op jit(solution)/shard_map/psum | solution.py:170
  265.5 64.9 %all-reduce.8 = (f32[]{:T(128)}, f32[]{:T(128)}) all-reduce(f32[]{:T(128)} %get-tuple-element.14, f32[]{:T(128)} %get-tuple-element.15), channel_id=1, replica_groups=mesh['gx'=8,'gy'=8,'gz'=4] {'gy','gz'}, use_global_device_ids=true, to_apply=%region_3.4 | all-reduce | flops 2 | bytes 16 | tf_op jit(solution)/shard_map/psum | solution.py:170
  335.0 4.4 collective-permute-start.24
  340.8 1.8 fusion.28
  345.9 81.3 %all-reduce.7 = f32[9216]{0:T(1024)} all-reduce(f32[9216]{0:T(1024)} %dynamic-update-slice.1), channel_id=1, replica_groups=mesh['gx'=8,'gy'=8,'gz'=4] {'gx','gy','gz'}, use_global_device_ids=true, to_apply=%add.7 | all-reduce | flops 9216 | bytes 73728
  429.4 4.1 collective-permute-start.26
  433.5 2.6 convolution_bitcast_fusion
  437.5 2.0 collective-permute-start.27
  443.2 2.5 collective-permute-start.28
  449.1 4.1 collective-permute-done.29
  453.9 1.7 fusion.1582
  457.2 1.6 fusion.1580
  459.1 1.7 fusion.1579
  464.4 2.1 fusion.1576
  470.2 5.6 collective-permute-start.30
  477.9 7.2 collective-permute-done.31
  485.3 3.7 collective-permute-start.32
  489.0 1.9 collective-permute-start.33
  490.9 3.3 collective-permute-done.33
  494.5 3.4 collective-permute-start.34
  499.3 3.7 collective-permute-done.34
  503.0 4.1 collective-permute-done.35
  509.8 24.7 %psum.60 = f32[]{:T(128)} all-reduce(f32[]{:T(128)} %get-tuple-element.20), channel_id=1, replica_groups=mesh['gx'=8,'gy'=8,'gz'=4] {'gx'}, use_global_device_ids=true, to_apply=%region_8.9 | all-reduce | flops 1 | bytes 8 | tf_op jit(solution)/shard_map/psum | solution.py:170
  534.5 65.5 %psum.61 = f32[]{:T(128)} all-reduce(f32[]{:T(128)} %psum.60), channel_id=1, replica_groups=mesh['gx'=8,'gy'=8,'gz'=4] {'gy','gz'}, use_global_device_ids=true, to_apply=%region_9.10 | all-reduce | flops 1 | bytes 8 | tf_op jit(solution)/shard_map/psum | solution.py:170
  601.3 3.3 collective-permute-start.36
  605.9 7.0 collective-permute-done.37
  613.0 1.9 collective-permute-start.38
  614.9 8.9 %collective-permute-start.39 = (f32[3,10,1,128]{3,2,1,0:T(1,128)S(1)}, f32[3,10,1,128]{3,2,1,0:T(1,128)S(1)}, u32[]{:S(2)}, u32[]{:S(2)}) collective-permute-start(f32[3,10,1,128]{3,2,1,0:T(1,128)S(1)} %get-tuple-element.252), channel_id=1, source_target_pairs={{4,0},{8,4},{12,8},{16,12},{20,16},{24,20},{28,24},{5,1},{9,5},{13... | collective-permute-start | bytes 46088 | tf_op jit(solution)/shard_map/ppermute | solution.py:30
  624.8 3.3 collective-permute-start.40
  629.6 6.4 collective-permute-done.41
  645.1 24.4 %psum.62 = f32[]{:T(128)} all-reduce(f32[]{:T(128)} %fusion.1594), channel_id=1, replica_groups=mesh['gx'=8,'gy'=8,'gz'=4] {'gx'}, use_global_device_ids=true, to_apply=%region_11.12 | all-reduce | flops 1 | bytes 8 | tf_op jit(solution)/shard_map/psum | solution.py:170
  669.6 67.3 %psum.63 = f32[]{:T(128)} all-reduce(f32[]{:T(128)} %psum.62), channel_id=1, replica_groups=mesh['gx'=8,'gy'=8,'gz'=4] {'gy','gz'}, use_global_device_ids=true, to_apply=%region_12.13 | all-reduce | flops 1 | bytes 8 | tf_op jit(solution)/shard_map/psum | solution.py:170
  (470 shorter events, 89.8 us)
Async XLA Ops:
  0.6 105.7 %copy-start = (f32[36,9216]{1,0:T(8,128)S(1)}, f32[36,9216]{1,0:T(8,128)}, u32[]{:S(2)}) copy-start(f32[36,9216]{1,0:T(8,128)} %param.9) | copy-start | bytes 3981316
  1.8 105.9 %copy-start.120 = (s32[8,8,128]{2,1,0:T(8,128)S(1)}, s32[8,8,128]{2,1,0:T(8,128)}, u32[]{:S(2)}) copy-start(s32[8,8,128]{2,1,0:T(8,128)} %param.8) | copy-start | bytes 98308
  1.8 107.3 %collective-permute-start.6 = (f32[2,8,128]{2,1,0:T(8,128)S(1)}, f32[2,8,128]{2,1,0:T(8,128)S(1)}, u32[]{:S(2)}, u32[]{:S(2)}) collective-permute-start(f32[2,8,128]{2,1,0:T(8,128)S(1)} %broadcast_in_dim.51), channel_id=1, source_target_pairs={{0,32},{32,64},{64,96},{96,128},{128,160},{160,192},{192,224},{1,3... | collective-permute-start | bytes 24584 | tf_op jit(solution)/shard_map/ppermute | solution.py:29
  11.7 97.4 %collective-permute-start.7 = (f32[2,8,128]{2,1,0:T(8,128)S(1)}, f32[2,8,128]{2,1,0:T(8,128)S(1)}, u32[]{:S(2)}, u32[]{:S(2)}) collective-permute-start(f32[2,8,128]{2,1,0:T(8,128)S(1)} %broadcast_in_dim.59), channel_id=1, source_target_pairs={{32,0},{64,32},{96,64},{128,96},{160,128},{192,160},{224,192},{33,... | collective-permute-start | bytes 24584 | tf_op jit(solution)/shard_map/ppermute | solution.py:30
  13.8 100.5 %collective-permute-start = (f32[3,1,8,128]{3,2,1,0:T(8,128)S(1)}, f32[3,1,8,128]{3,2,1,0:T(8,128)S(1)}, u32[]{:S(2)}, u32[]{:S(2)}) collective-permute-start(f32[3,1,8,128]{3,2,1,0:T(8,128)S(1)} %get-tuple-element.276), channel_id=1, source_target_pairs={{0,32},{32,64},{64,96},{96,128},{128,160},{160,192},{192,224},{1,3... | collective-permute-start | bytes 36872 | tf_op jit(solution)/shard_map/ppermute | solution.py:29
  21.6 92.7 %collective-permute-start.1 = (f32[3,1,8,128]{3,2,1,0:T(8,128)S(1)}, f32[3,1,8,128]{3,2,1,0:T(8,128)S(1)}, u32[]{:S(2)}, u32[]{:S(2)}) collective-permute-start(f32[3,1,8,128]{3,2,1,0:T(8,128)S(1)} %get-tuple-element.275), channel_id=1, source_target_pairs={{32,0},{64,32},{96,64},{128,96},{160,128},{192,160},{224,192},{33,... | collective-permute-start | bytes 36872 | tf_op jit(solution)/shard_map/ppermute | solution.py:30
  23.0 85.7 %copy-start.124 = (f32[8]{0:T(128)}, f32[8]{0:T(128)S(1)}, u32[]{:S(2)}) copy-start(f32[8]{0:T(128)S(1)} %multiply_add_fusion.115) | copy-start | bytes 100
  23.0 85.7 %copy-start.127 = (f32[128]{0:T(128)}, f32[128]{0:T(128)S(1)}, u32[]{:S(2)}) copy-start(f32[128]{0:T(128)S(1)} %multiply_add_fusion.114) | copy-start | bytes 1540
  109.1 5.2 collective-permute-start.8
  112.3 5.0 collective-permute-start.9
  117.4 7.8 %collective-permute-start.10 = (f32[12,12,2]{2,1,0:T(8,128)S(1)}, f32[12,12,2]{2,1,0:T(8,128)S(1)}, u32[]{:S(2)}, u32[]{:S(2)}) collective-permute-start(f32[12,12,2]{2,1,0:T(8,128)S(1)} %get-tuple-element.273), channel_id=1, source_target_pairs={{0,1},{1,2},{2,3},{4,5},{5,6},{6,7},{8,9},{9,10},{10,11},{12,13},{... | collective-permute-start | bytes 3464 | tf_op jit(solution)/shard_map/ppermute | solution.py:29
  119.6 5.7 collective-permute-start.11
  120.9 6.1 collective-permute-start.2
  123.2 5.0 collective-permute-start.3
  126.3 30.5 %copy-start.1 = (f32[10,10,130]{2,1,0:T(8,128)}, f32[10,10,130]{2,1,0:T(8,128)S(1)}, u32[]{:S(2)}) copy-start(f32[10,10,130]{2,1,0:T(8,128)S(1)} %get-tuple-element.87) | copy-start | bytes 156004
  126.3 30.5 %copy-start.3 = (f32[10,10,130]{2,1,0:T(8,128)}, f32[10,10,130]{2,1,0:T(8,128)S(1)}, u32[]{:S(2)}) copy-start(f32[10,10,130]{2,1,0:T(8,128)S(1)} %get-tuple-element.88) | copy-start | bytes 156004
  126.3 30.5 %copy-start.5 = (f32[10,10,130]{2,1,0:T(8,128)}, f32[10,10,130]{2,1,0:T(8,128)S(1)}, u32[]{:S(2)}) copy-start(f32[10,10,130]{2,1,0:T(8,128)S(1)} %get-tuple-element.89) | copy-start | bytes 156004
  126.3 30.5 %copy-start.7 = (f32[10,10,130]{2,1,0:T(8,128)}, f32[10,10,130]{2,1,0:T(8,128)S(1)}, u32[]{:S(2)}) copy-start(f32[10,10,130]{2,1,0:T(8,128)S(1)} %get-tuple-element.90) | copy-start | bytes 156004
  126.4 30.5 %copy-start.9 = (f32[10,10,130]{2,1,0:T(8,128)}, f32[10,10,130]{2,1,0:T(8,128)S(1)}, u32[]{:S(2)}) copy-start(f32[10,10,130]{2,1,0:T(8,128)S(1)} %get-tuple-element.91) | copy-start | bytes 156004
  126.4 30.5 %copy-start.15 = (f32[10,10,130]{2,1,0:T(8,128)}, f32[10,10,130]{2,1,0:T(8,128)S(1)}, u32[]{:S(2)}) copy-start(f32[10,10,130]{2,1,0:T(8,128)S(1)} %get-tuple-element.73) | copy-start | bytes 156004
  126.4 30.5 %copy-start.17 = (f32[10,10,130]{2,1,0:T(8,128)}, f32[10,10,130]{2,1,0:T(8,128)S(1)}, u32[]{:S(2)}) copy-start(f32[10,10,130]{2,1,0:T(8,128)S(1)} %get-tuple-element.74) | copy-start | bytes 156004
  126.4 30.5 %copy-start.19 = (f32[10,10,130]{2,1,0:T(8,128)}, f32[10,10,130]{2,1,0:T(8,128)S(1)}, u32[]{:S(2)}) copy-start(f32[10,10,130]{2,1,0:T(8,128)S(1)} %get-tuple-element.92) | copy-start | bytes 156004
  126.4 30.5 %copy-start.21 = (f32[10,10,130]{2,1,0:T(8,128)}, f32[10,10,130]{2,1,0:T(8,128)S(1)}, u32[]{:S(2)}) copy-start(f32[10,10,130]{2,1,0:T(8,128)S(1)} %get-tuple-element.93) | copy-start | bytes 156004
  126.4 32.2 %copy-start.33 = (f32[1,10,10,130]{3,2,1,0:T(8,128)}, f32[1,10,10,130]{3,2,1,0:T(8,128)S(1)}, u32[]{:S(2)}) copy-start(f32[1,10,10,130]{3,2,1,0:T(8,128)S(1)} %get-tuple-element.72) | copy-start | bytes 156004
  127.0 29.9 %copy-start.11 = (f32[10,10,130]{2,1,0:T(8,128)}, f32[10,10,130]{2,1,0:T(8,128)S(1)}, u32[]{:S(2)}) copy-start(f32[10,10,130]{2,1,0:T(8,128)S(1)} %get-tuple-element.95) | copy-start | bytes 156004
  127.0 29.9 %copy-start.13 = (f32[10,10,130]{2,1,0:T(8,128)}, f32[10,10,130]{2,1,0:T(8,128)S(1)}, u32[]{:S(2)}) copy-start(f32[10,10,130]{2,1,0:T(8,128)S(1)} %get-tuple-element.96) | copy-start | bytes 156004
  127.0 31.6 %copy-start.29 = (f32[1,10,10,130]{3,2,1,0:T(8,128)}, f32[1,10,10,130]{3,2,1,0:T(8,128)S(1)}, u32[]{:S(2)}) copy-start(f32[1,10,10,130]{3,2,1,0:T(8,128)S(1)} %get-tuple-element.94) | copy-start | bytes 156004
  128.4 7.7 %collective-permute-start.4 = (f32[3,10,10,1]{3,0,2,1:T(4,128)S(1)}, f32[3,10,10,1]{3,0,2,1:T(4,128)S(1)}, u32[]{:S(2)}, u32[]{:S(2)}) collective-permute-start(f32[3,10,10,1]{3,0,2,1:T(4,128)S(1)} %get-tuple-element.243), channel_id=1, source_target_pairs={{0,1},{1,2},{2,3},{4,5},{5,6},{6,7},{8,9},{9,10},{10,11},{12,13},{... | collective-permute-start | bytes 3608 | tf_op jit(solution)/shard_map/ppermute | solution.py:29
  132.7 7.5 %collective-permute-start.5 = (f32[3,10,10,1]{3,0,2,1:T(4,128)S(1)}, f32[3,10,10,1]{3,0,2,1:T(4,128)S(1)}, u32[]{:S(2)}, u32[]{:S(2)}) collective-permute-start(f32[3,10,10,1]{3,0,2,1:T(4,128)S(1)} %get-tuple-element.244), channel_id=1, source_target_pairs={{1,0},{2,1},{3,2},{5,4},{6,5},{7,6},{9,8},{10,9},{11,10},{13,12},{... | collective-permute-start | bytes 3608 | tf_op jit(solution)/shard_map/ppermute | solution.py:30
  159.1 6.9 collective-permute-start.12
  164.3 9.3 %collective-permute-start.13 = (f32[3,1,10,130]{3,2,1,0:T(8,128)S(1)}, f32[3,1,10,130]{3,2,1,0:T(8,128)S(1)}, u32[]{:S(2)}, u32[]{:S(2)}) collective-permute-start(f32[3,1,10,130]{3,2,1,0:T(8,128)S(1)} %get-tuple-element.110), channel_id=1, source_target_pairs={{32,0},{64,32},{96,64},{128,96},{160,128},{192,160},{224,192},{33,... | collective-permute-start | bytes 46808 | tf_op jit(solution)/shard_map/ppermute | solution.py:30
  166.0 73.9 %copy-start.110 = (f32[1,8192]{1,0:T(1,128)}, f32[1,8192]{1,0:T(1,128)S(1)}, u32[]{:S(2)}) copy-start(f32[1,8192]{1,0:T(1,128)S(1)} %get-tuple-element.228) | copy-start | bytes 98308
  166.0 73.9 %copy-start.112 = (f32[1,8192]{1,0:T(1,128)}, f32[1,8192]{1,0:T(1,128)S(1)}, u32[]{:S(2)}) copy-start(f32[1,8192]{1,0:T(1,128)S(1)} %get-tuple-element.229) | copy-start | bytes 98308
  166.0 73.9 %copy-start.114 = (f32[1,8192]{1,0:T(1,128)}, f32[1,8192]{1,0:T(1,128)S(1)}, u32[]{:S(2)}) copy-start(f32[1,8192]{1,0:T(1,128)S(1)} %get-tuple-element.230) | copy-start | bytes 98308
  173.8 5.9 collective-permute-start.14
  177.7 5.3 collective-permute-start.15
  183.3 7.6 %collective-permute-start.16 = (f32[3,12,12,1]{3,2,1,0:T(8,128)S(1)}, f32[3,12,12,1]{3,2,1,0:T(8,128)S(1)}, u32[]{:S(2)}, u32[]{:S(2)}) collective-permute-start(f32[3,12,12,1]{3,2,1,0:T(8,128)S(1)} %get-tuple-element.103), channel_id=1, source_target_pairs={{0,1},{1,2},{2,3},{4,5},{5,6},{6,7},{8,9},{9,10},{10,11},{12,13},{... | collective-permute-start | bytes 5192 | tf_op jit(solution)/shard_map/ppermute | solution.py:29
  185.8 9.2 %collective-permute-start.17 = (f32[3,12,12,1]{3,2,1,0:T(8,128)S(1)}, f32[3,12,12,1]{3,2,1,0:T(8,128)S(1)}, u32[]{:S(2)}, u32[]{:S(2)}) collective-permute-start(f32[3,12,12,1]{3,2,1,0:T(8,128)S(1)} %get-tuple-element.104), channel_id=1, source_target_pairs={{1,0},{2,1},{3,2},{5,4},{6,5},{7,6},{9,8},{10,9},{11,10},{13,12},{... | collective-permute-start | bytes 5192 | tf_op jit(solution)/shard_map/ppermute | solution.py:30
  197.7 42.3 %copy-start.101 = (f32[1,3,64,128]{3,2,1,0:T(8,128)}, f32[1,3,64,128]{3,2,1,0:T(8,128)S(1)}, u32[]{:S(2)}) copy-start(f32[1,3,64,128]{3,2,1,0:T(8,128)S(1)} %get-tuple-element.227) | copy-start | bytes 294916
  197.7 6.5 collective-permute-start.18
  202.9 8.8 %collective-permute-start.19 = (f32[3,1,8,128]{3,2,1,0:T(8,128)S(1)}, f32[3,1,8,128]{3,2,1,0:T(8,128)S(1)}, u32[]{:S(2)}, u32[]{:S(2)}) collective-permute-start(f32[3,1,8,128]{3,2,1,0:T(8,128)S(1)} %get-tuple-element.272), channel_id=1, source_target_pairs={{32,0},{64,32},{96,64},{128,96},{160,128},{192,160},{224,192},{33,... | collective-permute-start | bytes 36872 | tf_op jit(solution)/shard_map/ppermute | solution.py:30
  211.7 7.1 collective-permute-start.20
  216.9 5.0 collective-permute-start.21
  222.1 12.9 %collective-permute-start.22 = (f32[3,10,10,1]{3,0,2,1:T(4,128)S(1)}, f32[3,10,10,1]{3,0,2,1:T(4,128)S(1)}, u32[]{:S(2)}, u32[]{:S(2)}) collective-permute-start(f32[3,10,10,1]{3,0,2,1:T(4,128)S(1)} %get-tuple-element.241), channel_id=1, source_target_pairs={{0,1},{1,2},{2,3},{4,5},{5,6},{6,7},{8,9},{9,10},{10,11},{12,13},{... | collective-permute-start | bytes 3608 | tf_op jit(solution)/shard_map/ppermute | solution.py:29
  225.0 7.5 %collective-permute-start.23 = (f32[3,10,10,1]{3,0,2,1:T(4,128)S(1)}, f32[3,10,10,1]{3,0,2,1:T(4,128)S(1)}, u32[]{:S(2)}, u32[]{:S(2)}) collective-permute-start(f32[3,10,10,1]{3,0,2,1:T(4,128)S(1)} %get-tuple-element.242), channel_id=1, source_target_pairs={{1,0},{2,1},{3,2},{5,4},{6,5},{7,6},{9,8},{10,9},{11,10},{13,12},{... | collective-permute-start | bytes 3608 | tf_op jit(solution)/shard_map/ppermute | solution.py:30
  335.0 92.2 %collective-permute-start.24 = (f32[3,1,8,128]{3,2,1,0:T(8,128)}, f32[3,1,8,128]{3,2,1,0:T(8,128)}, u32[]{:S(2)}, u32[]{:S(2)}) collective-permute-start(f32[3,1,8,128]{3,2,1,0:T(8,128)} %get-tuple-element.269), channel_id=1, source_target_pairs={{0,32},{32,64},{64,96},{96,128},{128,160},{160,192},{192,224},{1,3... | collective-permute-start | bytes 36872 | tf_op jit(solution)/shard_map/ppermute | solution.py:29
  339.4 87.8 %collective-permute-start.25 = (f32[3,1,8,128]{3,2,1,0:T(8,128)}, f32[3,1,8,128]{3,2,1,0:T(8,128)}, u32[]{:S(2)}, u32[]{:S(2)}) collective-permute-start(f32[3,1,8,128]{3,2,1,0:T(8,128)} %get-tuple-element.270), channel_id=1, source_target_pairs={{32,0},{64,32},{96,64},{128,96},{160,128},{192,160},{224,192},{33,... | collective-permute-start | bytes 36872 | tf_op jit(solution)/shard_map/ppermute | solution.py:30
  429.4 10.1 %collective-permute-start.26 = (f32[3,10,1,128]{3,2,1,0:T(1,128)}, f32[3,10,1,128]{3,2,1,0:T(1,128)}, u32[]{:S(2)}, u32[]{:S(2)}) collective-permute-start(f32[3,10,1,128]{3,2,1,0:T(1,128)} %get-tuple-element.254), channel_id=1, source_target_pairs={{0,4},{4,8},{8,12},{12,16},{16,20},{20,24},{24,28},{1,5},{5,9},{9,... | collective-permute-start | bytes 46088 | tf_op jit(solution)/shard_map/ppermute | solution.py:29
  437.5 5.4 collective-permute-start.27
  443.2 5.9 collective-permute-start.28
  445.7 7.5 %collective-permute-start.29 = (f32[3,10,10,1]{3,0,2,1:T(4,128)S(1)}, f32[3,10,10,1]{3,0,2,1:T(4,128)S(1)}, u32[]{:S(2)}, u32[]{:S(2)}) collective-permute-start(f32[3,10,10,1]{3,0,2,1:T(4,128)S(1)} %get-tuple-element.240), channel_id=1, source_target_pairs={{1,0},{2,1},{3,2},{5,4},{6,5},{7,6},{9,8},{10,9},{11,10},{13,12},{... | collective-permute-start | bytes 3608 | tf_op jit(solution)/shard_map/ppermute | solution.py:30
  448.3 42.6 %copy-start.43 = (f32[6,8192]{1,0:T(8,128)}, f32[6,8192]{1,0:T(8,128)S(1)}, u32[]{:S(2)}) copy-start(f32[6,8192]{1,0:T(8,128)S(1)} %fusion.36) | copy-start | bytes 589828
  470.2 7.8 %collective-permute-start.30 = (f32[3,1,10,130]{3,2,1,0:T(8,128)S(1)}, f32[3,1,10,130]{3,2,1,0:T(8,128)S(1)}, u32[]{:S(2)}, u32[]{:S(2)}) collective-permute-start(f32[3,1,10,130]{3,2,1,0:T(8,128)S(1)} %get-tuple-element.107), channel_id=1, source_target_pairs={{0,32},{32,64},{64,96},{96,128},{128,160},{160,192},{192,224},{1,3... | collective-permute-start | bytes 46808 | tf_op jit(solution)/shard_map/ppermute | solution.py:29
  475.8 9.4 %collective-permute-start.31 = (f32[3,1,10,130]{3,2,1,0:T(8,128)S(1)}, f32[3,1,10,130]{3,2,1,0:T(8,128)S(1)}, u32[]{:S(2)}, u32[]{:S(2)}) collective-permute-start(f32[3,1,10,130]{3,2,1,0:T(8,128)S(1)} %get-tuple-element.108), channel_id=1, source_target_pairs={{32,0},{64,32},{96,64},{128,96},{160,128},{192,160},{224,192},{33,... | collective-permute-start | bytes 46808 | tf_op jit(solution)/shard_map/ppermute | solution.py:30
  485.3 5.7 collective-permute-start.32
  489.0 5.3 collective-permute-start.33
  494.5 8.5 %collective-permute-start.34 = (f32[3,12,12,1]{3,2,1,0:T(8,128)S(1)}, f32[3,12,12,1]{3,2,1,0:T(8,128)S(1)}, u32[]{:S(2)}, u32[]{:S(2)}) collective-permute-start(f32[3,12,12,1]{3,2,1,0:T(8,128)S(1)} %get-tuple-element.99), channel_id=1, source_target_pairs={{0,1},{1,2},{2,3},{4,5},{5,6},{6,7},{8,9},{9,10},{10,11},{12,13},{... | collective-permute-start | bytes 5192 | tf_op jit(solution)/shard_map/ppermute | solution.py:29
  497.9 9.2 %collective-permute-start.35 = (f32[3,12,12,1]{3,2,1,0:T(8,128)S(1)}, f32[3,12,12,1]{3,2,1,0:T(8,128)S(1)}, u32[]{:S(2)}, u32[]{:S(2)}) collective-permute-start(f32[3,12,12,1]{3,2,1,0:T(8,128)S(1)} %get-tuple-element.100), channel_id=1, source_target_pairs={{1,0},{2,1},{3,2},{5,4},{6,5},{7,6},{9,8},{10,9},{11,10},{13,12},{... | collective-permute-start | bytes 5192 | tf_op jit(solution)/shard_map/ppermute | solution.py:30
  601.3 4.6 collective-permute-start.36
  604.6 8.3 %collective-permute-start.37 = (f32[3,1,8,128]{3,2,1,0:T(8,128)S(1)}, f32[3,1,8,128]{3,2,1,0:T(8,128)S(1)}, u32[]{:S(2)}, u32[]{:S(2)}) collective-permute-start(f32[3,1,8,128]{3,2,1,0:T(8,128)S(1)} %get-tuple-element.268), channel_id=1, source_target_pairs={{32,0},{64,32},{96,64},{128,96},{160,128},{192,160},{224,192},{33,... | collective-permute-start | bytes 36872 | tf_op jit(solution)/shard_map/ppermute | solution.py:30
  613.0 10.8 %collective-permute-start.38 = (f32[3,10,1,128]{3,2,1,0:T(1,128)S(1)}, f32[3,10,1,128]{3,2,1,0:T(1,128)S(1)}, u32[]{:S(2)}, u32[]{:S(2)}) collective-permute-start(f32[3,10,1,128]{3,2,1,0:T(1,128)S(1)} %get-tuple-element.251), channel_id=1, source_target_pairs={{0,4},{4,8},{8,12},{12,16},{16,20},{20,24},{24,28},{1,5},{5,9},{9,... | collective-permute-start | bytes 46088 | tf_op jit(solution)/shard_map/ppermute | solution.py:29
  614.9 9.7 %collective-permute-start.39 = (f32[3,10,1,128]{3,2,1,0:T(1,128)S(1)}, f32[3,10,1,128]{3,2,1,0:T(1,128)S(1)}, u32[]{:S(2)}, u32[]{:S(2)}) collective-permute-start(f32[3,10,1,128]{3,2,1,0:T(1,128)S(1)} %get-tuple-element.252), channel_id=1, source_target_pairs={{4,0},{8,4},{12,8},{16,12},{20,16},{24,20},{28,24},{5,1},{9,5},{13... | collective-permute-start | bytes 46088 | tf_op jit(solution)/shard_map/ppermute | solution.py:30
  624.8 14.0 %collective-permute-start.40 = (f32[3,10,10,1]{3,0,2,1:T(4,128)S(1)}, f32[3,10,10,1]{3,0,2,1:T(4,128)S(1)}, u32[]{:S(2)}, u32[]{:S(2)}) collective-permute-start(f32[3,10,10,1]{3,0,2,1:T(4,128)S(1)} %get-tuple-element.237), channel_id=1, source_target_pairs={{0,1},{1,2},{2,3},{4,5},{5,6},{6,7},{8,9},{9,10},{10,11},{12,13},{... | collective-permute-start | bytes 3608 | tf_op jit(solution)/shard_map/ppermute | solution.py:29
  628.1 7.9 %collective-permute-start.41 = (f32[3,10,10,1]{3,0,2,1:T(4,128)S(1)}, f32[3,10,10,1]{3,0,2,1:T(4,128)S(1)}, u32[]{:S(2)}, u32[]{:S(2)}) collective-permute-start(f32[3,10,10,1]{3,0,2,1:T(4,128)S(1)} %get-tuple-element.238), channel_id=1, source_target_pairs={{1,0},{2,1},{3,2},{5,4},{6,5},{7,6},{9,8},{10,9},{11,10},{13,12},{... | collective-permute-start | bytes 3608 | tf_op jit(solution)/shard_map/ppermute | solution.py:30
  (108 other events, 610.7 us)
